TPU v7x, 32 devices: a whole 2x2x4 slice. The times are simulated.
32 devices in a mesh: path: 8 (over z, core), fsdp: 4 (over y, x).
Axes of the slice: x: 2, y: 2, z: 4, core: 2. Of those that a mesh axis runs over, the one named last changes fastest.
Arguments:
- path_delta: bfloat16 [8, 4, 128, 4096], P('path', None, 'fsdp'), may hold values from -20 to 20
- feedback: float32 [8, 4, 128, 4096], P('path', None, 'fsdp'), may hold values from -4 to 4
- global_params: float32 [4, 2, 128, 4096], P(None, None, 'fsdp', 'path'), may hold values from -0.09375 to 0.09375
- momentum: float32 [4, 2, 128, 4096], P(None, None, 'fsdp', 'path'), may hold values from -2 to 2
- routes: int32 [8, 4], replicated, may hold values from 0 to 1
- token_counts: int32 [8, 4], replicated, may hold values from 1 to 16
- skip_flags: int32 [4, 2], replicated, may hold values from 0 to 1, as said below
Outputs:
- feedback_next: float32 [8, 4, 128, 4096], P('path', None, 'fsdp')
- momentum_next: float32 [4, 2, 128, 4096], P(None, None, 'fsdp', 'path')
- params_next: float32 [4, 2, 128, 4096], P(None, None, 'fsdp', 'path')
- path_params: bfloat16 [8, 4, 128, 4096], P('path', None, 'fsdp')
Inputs may be any that keep to these rules, and one draw needn't show every extreme that they name: `skip_flags`: at most one of the two modules of a level skips.
All inputs are finite; a program needn't handle non-finite values.
Results may differ from a plain program's by a relative error of at most 0.012.
Values may be sent and summed in bfloat16 or wider, within the bound.
A program may use at most 64 MiB of HBM per device.

v0:
```python
import jax
import jax.numpy as jnp
from jax import lax
from jax.sharding import PartitionSpec as P

clip_rms = 0.2
outer_rate = 0.7
momentum_coef = 0.9
epsilon_sq = 1e-06


def on_device(path_delta, feedback, global_params, momentum, routes, token_counts, skip_flags):
    own_index = lax.axis_index("path")
    counts = token_counts.astype(jnp.float32)
    same = (routes[:, None, :] == routes[None, :, :]).astype(jnp.float32)
    denom = jnp.sum(same * counts[None, :, :], axis=1)
    weight = counts / denom
    skipped_path = jnp.where(routes == 1, skip_flags[None, :, 1], skip_flags[None, :, 0])
    live = (1 - skipped_path).astype(jnp.float32)
    own_weight = lax.dynamic_slice_in_dim(weight, own_index, 1, 0)[0]
    own_live = lax.dynamic_slice_in_dim(live, own_index, 1, 0)[0]
    own_route = lax.dynamic_slice_in_dim(routes, own_index, 1, 0)[0]
    corrected = path_delta[0].astype(jnp.float32) + feedback[0]
    scaled = (own_weight[:, None, None] * corrected).astype(jnp.bfloat16)
    sent = jnp.where(own_live[:, None, None] > 0, scaled, jnp.zeros_like(scaled))
    feedback_next = corrected - own_live[:, None, None] * (
        sent.astype(jnp.float32) / own_weight[:, None, None]
    )
    own_hot = (own_route[:, None] == jnp.arange(2, dtype=jnp.int32)[None, :]).astype(jnp.float32)
    terms = own_hot[:, :, None, None] * sent.astype(jnp.float32)[:, None]
    average = lax.psum_scatter(
        terms.astype(jnp.bfloat16), "path", scatter_dimension=3, tiled=True
    ).astype(jnp.float32)
    local_sq = jnp.sum(average * average, axis=(2, 3))
    total_sq = lax.psum(local_sq, ("path", "fsdp"))
    entries = average.shape[2] * average.shape[3] * lax.axis_size("path") * lax.axis_size("fsdp")
    factor = jnp.minimum(1.0, clip_rms / jnp.sqrt(total_sq / entries + epsilon_sq))
    clipped = factor[:, :, None, None] * average
    skipped = (skip_flags > 0)[:, :, None, None]
    momentum_next = jnp.where(skipped, momentum, momentum_coef * momentum + clipped)
    params_next = jnp.where(
        skipped,
        global_params,
        global_params - outer_rate * (clipped + momentum_coef * momentum_next),
    )
    narrow = params_next.astype(jnp.bfloat16)
    outgoing = jnp.where((routes == 1)[:, :, None, None], narrow[None, :, 1], narrow[None, :, 0])
    returned = lax.all_to_all(outgoing, "path", split_axis=0, concat_axis=3, tiled=True)
    return (feedback_next[None], momentum_next, params_next, returned)


def solution(mesh):
    return jax.shard_map(
        on_device,
        mesh=mesh,
        in_specs=(
            P("path", None, "fsdp", None),
            P("path", None, "fsdp", None),
            P(None, None, "fsdp", "path"),
            P(None, None, "fsdp", "path"),
            P(),
            P(),
            P(),
        ),
        out_specs=(
            P("path", None, "fsdp", None),
            P(None, None, "fsdp", "path"),
            P(None, None, "fsdp", "path"),
            P("path", None, "fsdp", None),
        ),
        check_vma=False,
    )
```

profile of v0, /device:TPU:1, one launch (start us, length us, event | category | flops | bytes accessed | tf_op | source)
XLA Modules:
  0.0 135.4 jit_solution(1709357491064695534)
XLA Ops:
  7.2 0.0 reduce-scatter.2.cloned.1.call-start
  7.2 0.8 slice_bitcast_fusion.3
  8.0 0.7 convert_element_type.55
  8.7 0.9 select_reduce_fusion
  9.6 0.7 convert_divide_fusion
  10.3 0.9 dynamic-slice_reduce_fusion
  11.1 0.8 subtract_convert_fusion
  11.9 0.2 dynamic-slice_reduce_fusion.1
  12.1 0.1 fusion.9
  12.2 2.3 %fusion.3 = f32[4,32,4096]{2,1,0:T(8,128)S(1)} fusion(f32[1,4,32,4096]{3,2,1,0:T(8,128)} %param.8, bf16[1,4,32,4096]{3,2,1,0:T(8,128)(2,1)} %param.7, f32[4]{0:T(128)S(1)} %get-tuple-element.13, pred[4]{0:T(512)(128)(4,1)S(1)} %broadcast_compare_fusion.2), kind=kLoop, calls=%fused_computation.8 | loop fusion | flops 3145728 | bytes 5242900 | tf_op jit(solution)/shard_map/convert_element_type | solution.py:27
  14.5 1.7 %multiply_convert_fusion = bf16[4,2,32,4096]{3,2,1,0:T(8,128)(2,1)} fusion(f32[4,32,4096]{2,1,0:T(8,128)S(1)} %fusion.3, f32[4,2]{1,0:T(4,128)S(1)} %fusion.9), kind=kLoop, calls=%fused_computation | loop fusion | flops 2097152 | bytes 4194336 | tf_op jit(solution)/shard_map/convert_element_type | solution.py:32
  16.2 0.0 copy-start.3
  16.2 0.0 copy-start.1
  16.2 0.0 copy-start.2
  16.2 0.0 reduce-scatter.2.cloned.1.call-update
  16.2 0.6 copy-done.3
  16.9 0.1 copy.29
  17.0 34.8 %reduce-scatter.2.cloned.1.call-done = bf16[4,2,32,512]{3,2,1,0:T(8,128)(2,1)} async-done(((bf16[4,2,32,4096]{3,2,1,0:T(8,128)(2,1)}), bf16[4,2,32,512]{3,2,1,0:T(8,128)(2,1)}) %reduce-scatter.2.cloned.1.call-update) | async-done | bytes 262160 | tf_op jit(solution)/shard_map/reduce_scatter | solution.py:31
  51.8 1.1 fusion.8
  52.9 0.1 copy.30
  53.0 39.7 %psum.7 = f32[4,2]{1,0:T(4,128)S(1)} all-reduce(f32[4,2]{1,0:T(4,128)S(1)} %fusion.8), channel_id=1, replica_groups=mesh['path'=8,'fsdp'=4] {'path','fsdp'}, use_global_device_ids=true, to_apply=%region_3.4 | all-reduce | flops 8 | bytes 64 | tf_op jit(solution)/shard_map/psum | solution.py:35
  92.7 0.0 copy-done.1
  92.7 0.0 copy-done.2
  92.7 2.3 %fusion.10 = (bf16[4,2,32,512]{3,2,1,0:T(8,128)(2,1)S(1)}, f32[4,2,32,512]{3,2,1,0:T(8,128)}, f32[4,2,32,512]{3,2,1,0:T(8,128)}) fusion(f32[4,2,32,512]{3,2,1,0:T(8,128)S(1)} %copy-done.1, bf16[4,2,32,512]{3,2,1,0:T(8,128)(2,1)} %reduce-scatter.2.cloned.1.call-done, f32[4,2]{1,0:T(4,128)S(1)} %multiply_minimum_fusion, pred[4,2]{1,0:T(4,128)(4,1)S(1)} %copy.29, ...), kind=kLoop, calls=%fused_computation.34 | loop fusion | flops 1441792 | bytes 2621480 | tf_op jit(solution)/shard_map/convert_element_type | solution.py:46
  95.0 0.0 copy-start
  95.0 1.1 broadcast_select_fusion
  96.1 5.7 %all-to-all-start = ((bf16[8,4,32,512]{3,2,1,0:T(8,128)(2,1)}), bf16[8,4,32,512]{3,2,1,0:T(8,128)(2,1)S(1)}, u32[]{:S(2)}, u32[]{:S(2)}) async-start(bf16[8,4,32,512]{3,2,1,0:T(8,128)(2,1)} %broadcast_select_fusion), calls=%async_computation.1 | async-start | bytes 2097152 | tf_op jit(solution)/shard_map/all_to_all | solution.py:48
  101.8 0.0 copy-done
  101.8 3.1 %multiply_subtract_fusion = f32[1,4,32,4096]{3,2,1,0:T(8,128)} fusion(f32[1,4,32,4096]{3,2,1,0:T(8,128)S(1)} %copy-done, bf16[1,4,32,4096]{3,2,1,0:T(8,128)(2,1)} %param.7, f32[4]{0:T(128)S(1)} %get-tuple-element.13, f32[4]{0:T(128)S(1)} %get-tuple-element.14, pred[4]{0:T(512)(128)(4,1)S(1)} %broadcast_compare_fusion.2), kind=kLoop, calls=%fused_computation.3 | loop fusion | flops 4718592 | bytes 5242916 | tf_op jit(solution)/shard_map/sub | solution.py:26
  104.9 22.5 %all-to-all-done = bf16[8,4,32,512]{3,2,1,0:T(8,128)(2,1)S(1)} async-done(((bf16[8,4,32,512]{3,2,1,0:T(8,128)(2,1)}), bf16[8,4,32,512]{3,2,1,0:T(8,128)(2,1)S(1)}, u32[]{:S(2)}, u32[]{:S(2)}) %all-to-all-start) | async-done | bytes 1048608 | tf_op jit(solution)/shard_map/all_to_all | solution.py:48
  127.4 1.1 copy.32
  (4 shorter events, 0.0 us)
Async XLA Ops:
  7.2 44.6 %reduce-scatter.2.cloned.1.call-start = ((), (), s32[]{:S(2)}) async-start(), calls=%async_computation.2 | async-start | bytes 2359296 | tf_op jit(solution)/shard_map/reduce_scatter | solution.py:31
  16.2 0.7 copy-start.3
  16.2 76.6 %copy-start.1 = (f32[4,2,32,512]{3,2,1,0:T(8,128)S(1)}, f32[4,2,32,512]{3,2,1,0:T(8,128)}, u32[]{:S(2)}) copy-start(f32[4,2,32,512]{3,2,1,0:T(8,128)} %param.9) | copy-start | bytes 1572868
  16.2 76.6 %copy-start.2 = (f32[4,2,32,512]{3,2,1,0:T(8,128)S(1)}, f32[4,2,32,512]{3,2,1,0:T(8,128)}, u32[]{:S(2)}) copy-start(f32[4,2,32,512]{3,2,1,0:T(8,128)} %param.10) | copy-start | bytes 1572868
  95.0 6.8 %copy-start = (f32[1,4,32,4096]{3,2,1,0:T(8,128)S(1)}, f32[1,4,32,4096]{3,2,1,0:T(8,128)}, u32[]{:S(2)}) copy-start(f32[1,4,32,4096]{3,2,1,0:T(8,128)} %param.8) | copy-start | bytes 6291460
  96.1 31.3 %all-to-all-start = ((bf16[8,4,32,512]{3,2,1,0:T(8,128)(2,1)}), bf16[8,4,32,512]{3,2,1,0:T(8,128)(2,1)S(1)}, u32[]{:S(2)}, u32[]{:S(2)}) async-start(bf16[8,4,32,512]{3,2,1,0:T(8,128)(2,1)} %broadcast_select_fusion), calls=%async_computation.1 | async-start | bytes 2097152 | tf_op jit(solution)/shard_map/all_to_all | solution.py:48
Sparse Core Ops, SparseCore 0:
  16.3 35.4 reduce-scatter.1
where the time goes:
time: 137 us; the launch traced here: 135 us
  waiting for transfers between devices  57.4 us (42%)
  blocking collectives  39.7 us (29%)
  other arithmetic  14.6 us (11%)
  between operations  14.1 us (10%)
  starting transfers between devices  5.74 us (4%)
  local copies, waits for them, and re-layouts  3.82 us (3%)
    psum x1, blocking collectives, on_device(): total_sq = lax.psum(local_sq, ('path', 'fsdp'))  39.7 us
    reduce_scatter x1, waiting for transfers between devices, on_device(): lax.psum_scatter(terms.astype(jnp.bfloat16), 'path', scatter_dimension=3,...  34.8 us
    all_to_all x1, waiting for transfers between devices, on_device(): lax.all_to_all(outgoing, 'path', split_axis=0, concat_axis=3, tiled=True)  22.5 us
    all_to_all x1, starting transfers between devices, on_device(): lax.all_to_all(outgoing, 'path', split_axis=0, concat_axis=3, tiled=True)  5.71 us
    sub x1, other arithmetic, on_device(): corrected - own_live[:, None, None] * (sent.astype(jnp.float32) / own_wei...  3.06 us
  transfers between devices with their start and end apart: 2, of which 2 were waited for; matrix products, arithmetic and copies ran while one was open for 2% of the time, Pallas kernels for 0%

commit v1 on v0

v1 whole, which is shorter than its diff:
```python
import functools

import jax
import jax.numpy as jnp
from jax import lax
from jax.experimental import pallas as pl
from jax.experimental.pallas import tpu as pltpu
from jax.sharding import PartitionSpec as P

clip_rms = 0.2
outer_rate = 0.7
momentum_coef = 0.9
epsilon_sq = 1e-06
MESH = pl.DeviceIdType.MESH


def kernel(
    n, f,
    routes, counts, skips, delta_hbm, feed_hbm, params_hbm, mom_hbm,
    feed_out, mom_out, params_out, path_out,
    delta, feed, params, mom, sent, recv, average, chosen, gathered,
    square, square_in, part, part_in,
    load_sem, store_sem, send1, recv1, send2, recv2, sendf, recvf, sendp, recvp,
):
    levels, rows, depth = delta.shape
    cols = depth // n
    me = lax.axis_index("path")
    mf = lax.axis_index("fsdp")
    entries = rows * cols * n * f

    loads = []
    for l in range(levels):
        pair = (
            pltpu.make_async_copy(delta_hbm.at[0, l], delta.at[l], load_sem.at[0, l]),
            pltpu.make_async_copy(feed_hbm.at[0, l], feed.at[l], load_sem.at[1, l]),
        )
        for copy in pair:
            copy.start()
        loads.append(pair)
    load_params = pltpu.make_async_copy(params_hbm, params, load_sem.at[2, 0])
    load_mom = pltpu.make_async_copy(mom_hbm, mom, load_sem.at[3, 0])
    load_params.start()
    load_mom.start()

    barrier = pltpu.get_barrier_semaphore()
    for k in range(1, n):
        pl.semaphore_signal(barrier, inc=1, device_id={"path": lax.rem(me + k, n)}, device_id_type=MESH)
    for k in range(1, f):
        pl.semaphore_signal(barrier, inc=1, device_id={"fsdp": lax.rem(mf + k, f)}, device_id_type=MESH)

    inverse = []
    for l in range(levels):
        own_route = routes[me, l]
        total = jnp.int32(0)
        for q in range(n):
            total = total + jnp.where(routes[q, l] == own_route, counts[q, l], 0)
        live = 1 - jnp.where(own_route == 1, skips[l, 1], skips[l, 0])
        top = jnp.full((1, 128), (counts[me, l] * live).astype(jnp.float32))
        own = jnp.full((1, 128), counts[me, l].astype(jnp.float32))
        bottom = jnp.full((1, 128), total.astype(jnp.float32))
        weight = (top / bottom)[0:1, 0:1]
        inverse.append((bottom / own)[0:1, 0:1])
        for copy in loads[l]:
            copy.wait()
        for r in range(0, rows, 16):
            corrected = delta[l, r : r + 16, :].astype(jnp.float32) + feed[l, r : r + 16, :]
            sent[l, r : r + 16, :] = (weight * corrected).astype(jnp.bfloat16)
        if l == 0:
            pl.semaphore_wait(barrier, n - 1 + f - 1)
        for k in range(1, n):
            peer = lax.rem(me + k, n)
            pltpu.make_async_remote_copy(
                sent.at[l, :, pl.ds(pl.multiple_of(peer * cols, cols), cols)],
                recv.at[l, me],
                send1.at[l, k],
                recv1.at[l, me],
                device_id={"path": peer},
                device_id_type=MESH,
            ).start()

    stores = []
    for l in range(levels):
        for r in range(0, rows, 16):
            corrected = delta[l, r : r + 16, :].astype(jnp.float32) + feed[l, r : r + 16, :]
            feed[l, r : r + 16, :] = corrected - sent[l, r : r + 16, :].astype(jnp.float32) * inverse[l]
        copy = pltpu.make_async_copy(feed.at[l], feed_out.at[0, l], store_sem.at[0, l])
        copy.start()
        stores.append(copy)

    mine = pl.ds(pl.multiple_of(me * cols, cols), cols)

    def waiting1(l, k):
        source = lax.rem(me + k, n)
        return pltpu.make_async_remote_copy(
            sent.at[l, :, pl.ds(pl.multiple_of(source * cols, cols), cols)],
            recv.at[l, source], send1.at[l, k], recv1.at[l, source],
            device_id={"path": source}, device_id_type=MESH,
        )

    def small(l, k, axis, at, size, src, dst, send, arrive, slot):
        peer = lax.rem(at + k, size)
        return pltpu.make_async_remote_copy(
            src.at[l], dst.at[l, at if slot is None else peer], send.at[l, k],
            arrive.at[l, at if slot is None else peer],
            device_id={axis: peer}, device_id_type=MESH,
        )

    fsdp_copy = lambda l, k, slot: small(l, k, "fsdp", mf, f, square, square_in, sendf, recvf, slot)
    path_copy = lambda l, k, slot: small(l, k, "path", me, n, part, part_in, sendp, recvp, slot)

    def reduce_level(l):
        for k in range(1, n):
            waiting1(l, k).wait_recv()
        own = sent[l, :, mine].astype(jnp.float32)
        own_upper = routes[me, l] == 1
        zero = jnp.zeros_like(own)
        first = jnp.where(own_upper, zero, own)
        second = jnp.where(own_upper, own, zero)
        for k in range(1, n):
            source = lax.rem(me + k, n)
            upper = routes[source, l] == 1
            block = recv[l, source].astype(jnp.float32)
            first = first + jnp.where(upper, zero, block)
            second = second + jnp.where(upper, block, zero)
        for m, value in enumerate((first, second)):
            average[l, m] = value
            lanes = jnp.sum(value * value, axis=0, keepdims=True)
            folded = lanes[:, 0:128]
            for c in range(128, cols, 128):
                folded = folded + lanes[:, c : c + 128]
            square[l, m : m + 1, :] = folded
        for k in range(1, f):
            fsdp_copy(l, k, None).start()

    def share_level(l):
        total = square[l]
        for k in range(1, f):
            fsdp_copy(l, k, 1).wait_recv()
            total = total + square_in[l, lax.rem(mf + k, f)]
        part[l] = total
        for k in range(1, n):
            path_copy(l, k, None).start()

    def update_level(l):
        total = part[l]
        for k in range(1, n):
            path_copy(l, k, 1).wait_recv()
            total = total + part_in[l, lax.rem(me + k, n)]
        mean = jnp.sum(total, axis=1, keepdims=True) / entries
        factor = jnp.minimum(1.0, clip_rms / jnp.sqrt(mean + epsilon_sq))
        narrow = []
        for m in range(2):
            skipped = skips[l, m] > 0
            clipped = factor[m : m + 1, :] * average[l, m]
            momentum = mom[l, m]
            old = params[l, m]
            momentum = jnp.where(skipped, momentum, momentum_coef * momentum + clipped)
            new = jnp.where(skipped, old, old - outer_rate * (clipped + momentum_coef * momentum))
            mom[l, m] = momentum
            params[l, m] = new
            narrow.append(new.astype(jnp.bfloat16))
        for k in range(1, n):
            peer = lax.rem(me + k, n)
            chosen[l, k] = jnp.where(routes[peer, l] == 1, narrow[1], narrow[0])
            pltpu.make_async_remote_copy(
                chosen.at[l, k], gathered.at[l, :, mine], send2.at[l, k], recv2.at[l, me],
                device_id={"path": peer}, device_id_type=MESH,
            ).start()
        gathered[l, :, mine] = jnp.where(routes[me, l] == 1, narrow[1], narrow[0])
        for index, (src, dst) in enumerate(((mom, mom_out), (params, params_out))):
            copy = pltpu.make_async_copy(src.at[l], dst.at[l], store_sem.at[1 + index, l])
            copy.start()
            stores.append(copy)

    load_params.wait()
    load_mom.wait()
    for step in range(levels + 2):
        if step < levels:
            reduce_level(step)
        if 0 <= step - 1 < levels:
            share_level(step - 1)
        if 0 <= step - 2 < levels:
            update_level(step - 2)

    def waiting2(l, k):
        source = lax.rem(me + k, n)
        return pltpu.make_async_remote_copy(
            chosen.at[l, k], gathered.at[l, :, pl.ds(pl.multiple_of(source * cols, cols), cols)],
            send2.at[l, k], recv2.at[l, source], device_id={"path": source}, device_id_type=MESH,
        )

    for l in range(levels):
        for k in range(1, n):
            waiting2(l, k).wait_recv()
        copy = pltpu.make_async_copy(gathered.at[l], path_out.at[0, l], store_sem.at[3, l])
        copy.start()
        stores.append(copy)
    for l in range(levels):
        for k in range(1, n):
            waiting1(l, k).wait_send()
            waiting2(l, k).wait_send()
            path_copy(l, k, 1).wait_send()
        for k in range(1, f):
            fsdp_copy(l, k, 1).wait_send()
    for copy in stores:
        copy.wait()


def on_device(n, f, path_delta, feedback, global_params, momentum, routes, token_counts, skip_flags):
    _, levels, rows, depth = path_delta.shape
    cols = depth // n
    smem = pl.BlockSpec(memory_space=pltpu.SMEM)
    anywhere = pl.BlockSpec(memory_space=pl.ANY)
    shape = jax.ShapeDtypeStruct
    dma = pltpu.SemaphoreType.DMA
    bf16, f32 = jnp.bfloat16, jnp.float32
    return pl.pallas_call(
        functools.partial(kernel, n, f),
        out_shape=(
            shape(feedback.shape, f32),
            shape(momentum.shape, f32),
            shape(global_params.shape, f32),
            shape(path_delta.shape, bf16),
        ),
        in_specs=[smem] * 3 + [anywhere] * 4,
        out_specs=(anywhere,) * 4,
        scratch_shapes=[
            pltpu.VMEM((levels, rows, depth), bf16),
            pltpu.VMEM((levels, rows, depth), f32),
            pltpu.VMEM(global_params.shape, f32),
            pltpu.VMEM(global_params.shape, f32),
            pltpu.VMEM((levels, rows, depth), bf16),
            pltpu.VMEM((levels, n, rows, cols), bf16),
            pltpu.VMEM(global_params.shape, f32),
            pltpu.VMEM((levels, n, rows, cols), bf16),
            pltpu.VMEM((levels, rows, depth), bf16),
            pltpu.VMEM((levels, 2, 128), f32),
            pltpu.VMEM((levels, f, 2, 128), f32),
            pltpu.VMEM((levels, 2, 128), f32),
            pltpu.VMEM((levels, n, 2, 128), f32),
            dma((4, levels)),
            dma((4, levels)),
            dma((levels, n)),
            dma((levels, n)),
            dma((levels, n)),
            dma((levels, n)),
            dma((levels, f)),
            dma((levels, f)),
            dma((levels, n)),
            dma((levels, n)),
        ],
        compiler_params=pltpu.CompilerParams(collective_id=0, has_side_effects=True),
    )(routes, token_counts, skip_flags, path_delta, feedback, global_params, momentum)


def solution(mesh):
    return jax.shard_map(
        functools.partial(on_device, mesh.shape["path"], mesh.shape["fsdp"]),
        mesh=mesh,
        in_specs=(
            P("path", None, "fsdp", None),
            P("path", None, "fsdp", None),
            P(None, None, "fsdp", "path"),
            P(None, None, "fsdp", "path"),
            P(),
            P(),
            P(),
        ),
        out_specs=(
            P("path", None, "fsdp", None),
            P(None, None, "fsdp", "path"),
            P(None, None, "fsdp", "path"),
            P("path", None, "fsdp", None),
        ),
        check_vma=False,
    )
```

time: 137 us -> 68.9 us (0.50)
  waiting for transfers between devices: 57.4 us -> 0 us
  Pallas kernels: 0 us -> 57.2 us
  blocking collectives: 39.7 us -> 0 us
  other arithmetic: 14.6 us -> 0 us
  between operations: 14.1 us -> 0.66 us
  local copies, waits for them, and re-layouts: 3.82 us -> 9.8 us
  starting transfers between devices: 5.74 us -> 0 us
    pallas_call x0 -> x1, Pallas kernels: none -> 57.2 us  [on_device(): pl.pallas_call(functools.partial(kernel, n, f), out_shape=(shape(feedback...]
    psum x1 -> x0, blocking collectives: 39.7 us -> none  [on_device(): total_sq = lax.psum(local_sq, ('path', 'fsdp'))]
    reduce_scatter x1 -> x0, waiting for transfers between devices: 34.8 us -> none  [on_device(): lax.psum_scatter(terms.astype(jnp.bfloat16), 'path', scatter_dimension=3,...]
    all_to_all x1 -> x0, waiting for transfers between devices: 22.5 us -> none  [on_device(): lax.all_to_all(outgoing, 'path', split_axis=0, concat_axis=3, tiled=True)]
    unnamed x8 -> x13, local copies, waits for them, and re-layouts: 0.66 us -> 9.8 us
    convert_element_type x6 -> x0, other arithmetic: 7.75 us -> none  [the longest x1 2.27 us: on_device(): sent.astype(jnp.float32) / own_weight[:, None, None]]
    all_to_all x1 -> x0, starting transfers between devices: 5.71 us -> none  [on_device(): lax.all_to_all(outgoing, 'path', split_axis=0, concat_axis=3, tiled=True)]
    sub x1 -> x0, other arithmetic: 3.06 us -> none  [on_device(): corrected - own_live[:, None, None] * (sent.astype(jnp.float32) / own_wei...]
  transfers between devices with their start and end apart: 2 -> 0, of which waited for: 2 -> 0; matrix products, arithmetic and copies ran while one was open for 2% -> 0% of each run, Pallas kernels for 0% -> 0%
where the time goes in v1:
time: 68.9 us; the launch traced here: 67.7 us
  Pallas kernels  57.2 us (83%)
  local copies, waits for them, and re-layouts  9.8 us (14%)
    pallas_call x1, Pallas kernels, on_device(): pl.pallas_call(functools.partial(kernel, n, f), out_shape=(shape(feedback...  57.2 us
    unnamed x13, local copies, waits for them, and re-layouts  9.8 us

profile of v1, /device:TPU:1, one launch (start us, length us, event | category | flops | bytes accessed | tf_op | source)
XLA Modules:
  0.0 67.7 jit_solution(1190997806180787288)
XLA Ops:
  0.6 1.3 %copy.13.skips = s32[4,2]{1,0:T(4,128)} copy(s32[4,2]{0,1:T(2,128)} %param.13) | data formatting | bytes 64 | tf_op args[6]
  2.0 1.3 %copy.11.routes = s32[8,4]{1,0:T(8,128)} copy(s32[8,4]{0,1:T(4,128)} %param.11) | data formatting | bytes 256 | tf_op args[4]
  3.3 1.3 %copy.12.counts = s32[8,4]{1,0:T(8,128)} copy(s32[8,4]{0,1:T(4,128)} %param.12) | data formatting | bytes 256 | tf_op args[5]
  4.7 57.2 %shard_map.102 = (f32[1,4,32,4096]{3,2,1,0:T(8,128)}, f32[4,2,32,512]{3,2,1,0:T(8,128)}, f32[4,2,32,512]{3,2,1,0:T(8,128)}, bf16[1,4,32,4096]{3,2,1,0:T(8,128)(2,1)}) custom-call(s32[8,4]{1,0:T(8,128)} %copy.11.routes, s32[8,4]{1,0:T(8,128)} %copy.12.counts, s32[4,2]{1,0:T(4,128)} %copy.13.skips, bf16[1,4,32,4096]{3,2,1,0:T(8,128)(2,1)} %delta_hbm.1, ...), custom_call_target="tpu_custom_call" | custom-call | tf_op jit(solution)/shard_map/pallas_call | solution.py:217
  61.9 0.0 copy-start.2
  61.9 0.0 copy-start.1
  61.9 3.2 %copy.18 = f32[1,4,32,4096]{3,2,1,0:T(8,128)} copy(f32[1,4,32,4096]{3,2,1,0:T(8,128)} %get-tuple-element.8) | data formatting | bytes 4194304
  65.1 0.0 copy-done.2
  65.1 0.0 copy-start
  65.1 0.8 %copy.19 = f32[4,2,32,512]{3,2,1,0:T(8,128)} copy(f32[4,2,32,512]{3,2,1,0:T(8,128)S(1)} %copy-done.2) | data formatting | bytes 1048576
  65.9 0.0 copy-done.1
  65.9 0.8 %copy.20 = f32[4,2,32,512]{3,2,1,0:T(8,128)} copy(f32[4,2,32,512]{3,2,1,0:T(8,128)S(1)} %copy-done.1) | data formatting | bytes 1048576
  66.7 0.0 copy-done
  66.7 1.0 %copy.21 = bf16[1,4,32,4096]{3,2,1,0:T(8,128)(2,1)} copy(bf16[1,4,32,4096]{3,2,1,0:T(8,128)(2,1)S(1)} %copy-done) | data formatting | bytes 2097152
Async XLA Ops:
  61.9 3.2 %copy-start.2 = (f32[4,2,32,512]{3,2,1,0:T(8,128)S(1)}, f32[4,2,32,512]{3,2,1,0:T(8,128)}, u32[]{:S(2)}) copy-start(f32[4,2,32,512]{3,2,1,0:T(8,128)} %get-tuple-element.9) | copy-start | bytes 1572868
  61.9 4.0 %copy-start.1 = (f32[4,2,32,512]{3,2,1,0:T(8,128)S(1)}, f32[4,2,32,512]{3,2,1,0:T(8,128)}, u32[]{:S(2)}) copy-start(f32[4,2,32,512]{3,2,1,0:T(8,128)} %get-tuple-element.10) | copy-start | bytes 1572868
  65.1 1.6 %copy-start = (bf16[1,4,32,4096]{3,2,1,0:T(8,128)(2,1)S(1)}, bf16[1,4,32,4096]{3,2,1,0:T(8,128)(2,1)}, u32[]{:S(2)}) copy-start(bf16[1,4,32,4096]{3,2,1,0:T(8,128)(2,1)} %get-tuple-element.11) | copy-start | bytes 3145732

commit v2 on v1

--- a/solution.py
+++ b/solution.py
@@ -18,9 +18,9 @@
     n, f,
     routes, counts, skips, delta_hbm, feed_hbm, params_hbm, mom_hbm,
     feed_out, mom_out, params_out, path_out,
-    delta, feed, params, mom, sent, recv, average, chosen, gathered,
+    delta, feed, params, mom, sent, recv, average, blocks, gathered,
     square, square_in, part, part_in,
-    load_sem, store_sem, send1, recv1, send2, recv2, sendf, recvf, sendp, recvp,
+    load_sem, store_sem, send1, recv1, send_up, send_down, send_cross, recv2, sendf, recvf, sendp, recvp,
 ):
     levels, rows, depth = delta.shape
     cols = depth // n
@@ -50,13 +50,13 @@
 
     inverse = []
     for l in range(levels):
-        own_route = routes[me, l]
+        own_route = routes[l, me]
         total = jnp.int32(0)
         for q in range(n):
-            total = total + jnp.where(routes[q, l] == own_route, counts[q, l], 0)
-        live = 1 - jnp.where(own_route == 1, skips[l, 1], skips[l, 0])
-        top = jnp.full((1, 128), (counts[me, l] * live).astype(jnp.float32))
-        own = jnp.full((1, 128), counts[me, l].astype(jnp.float32))
+            total = total + jnp.where(routes[l, q] == own_route, counts[l, q], 0)
+        live = 1 - jnp.where(own_route == 1, skips[1, l], skips[0, l])
+        top = jnp.full((1, 128), (counts[l, me] * live).astype(jnp.float32))
+        own = jnp.full((1, 128), counts[l, me].astype(jnp.float32))
         bottom = jnp.full((1, 128), total.astype(jnp.float32))
         weight = (top / bottom)[0:1, 0:1]
         inverse.append((bottom / own)[0:1, 0:1])
@@ -112,13 +112,13 @@
         for k in range(1, n):
             waiting1(l, k).wait_recv()
         own = sent[l, :, mine].astype(jnp.float32)
-        own_upper = routes[me, l] == 1
+        own_upper = routes[l, me] == 1
         zero = jnp.zeros_like(own)
         first = jnp.where(own_upper, zero, own)
         second = jnp.where(own_upper, own, zero)
         for k in range(1, n):
             source = lax.rem(me + k, n)
-            upper = routes[source, l] == 1
+            upper = routes[l, source] == 1
             block = recv[l, source].astype(jnp.float32)
             first = first + jnp.where(upper, zero, block)
             second = second + jnp.where(upper, block, zero)
@@ -141,6 +141,58 @@
         for k in range(1, n):
             path_copy(l, k, None).start()
 
+    z, core = lax.div(me, 2), lax.rem(me, 2)
+    chips = n // 2
+
+    def along_copy(l, owner, up):
+        slot = 2 * owner + core
+        return pltpu.make_async_remote_copy(
+            blocks.at[l, slot], blocks.at[l, slot],
+            (send_up if up else send_down).at[l, owner], recv2.at[l, slot],
+            device_id={"path": me + 2 if up else me - 2}, device_id_type=MESH,
+        )
+
+    def cross_copy(l, owner):
+        slot = 2 * owner + core
+        return pltpu.make_async_remote_copy(
+            blocks.at[l, slot], blocks.at[l, slot], send_cross.at[l, owner], recv2.at[l, slot],
+            device_id={"path": me + 1 - 2 * core}, device_id_type=MESH,
+        )
+
+    def send_along(l, owner, up):
+        @pl.when(z + 1 < chips if up else z > 0)
+        def _():
+            along_copy(l, owner, up).start()
+
+    def arrived(l, slot):
+        pltpu.make_async_remote_copy(
+            blocks.at[l, slot], blocks.at[l, slot], send_cross.at[l, z], recv2.at[l, slot],
+            device_id={"path": me + 1 - 2 * core}, device_id_type=MESH,
+        ).wait_recv()
+
+    def relay(l, d):
+        @pl.when(z - d >= 0)
+        def _():
+            arrived(l, 2 * (z - d) + core)
+            send_along(l, z - d, True)
+            cross_copy(l, z - d).start()
+
+        @pl.when(z + d < chips)
+        def _():
+            arrived(l, 2 * (z + d) + core)
+            send_along(l, z + d, False)
+            cross_copy(l, z + d).start()
+
+    def finish_level(l):
+        for owner in range(chips):
+            arrived(l, 2 * owner + 1 - core)
+        upper = routes[l, me] == 1
+        for slot in range(n):
+            gathered[l, :, slot * cols : (slot + 1) * cols] = jnp.where(upper, blocks[l, slot, 1], blocks[l, slot, 0])
+        copy = pltpu.make_async_copy(gathered.at[l], path_out.at[0, l], store_sem.at[3, l])
+        copy.start()
+        stores.append(copy)
+
     def update_level(l):
         total = part[l]
         for k in range(1, n):
@@ -150,7 +202,7 @@
         factor = jnp.minimum(1.0, clip_rms / jnp.sqrt(mean + epsilon_sq))
         narrow = []
         for m in range(2):
-            skipped = skips[l, m] > 0
+            skipped = skips[m, l] > 0
             clipped = factor[m : m + 1, :] * average[l, m]
             momentum = mom[l, m]
             old = params[l, m]
@@ -159,14 +211,11 @@
             mom[l, m] = momentum
             params[l, m] = new
             narrow.append(new.astype(jnp.bfloat16))
-        for k in range(1, n):
-            peer = lax.rem(me + k, n)
-            chosen[l, k] = jnp.where(routes[peer, l] == 1, narrow[1], narrow[0])
-            pltpu.make_async_remote_copy(
-                chosen.at[l, k], gathered.at[l, :, mine], send2.at[l, k], recv2.at[l, me],
-                device_id={"path": peer}, device_id_type=MESH,
-            ).start()
-        gathered[l, :, mine] = jnp.where(routes[me, l] == 1, narrow[1], narrow[0])
+        for m in range(2):
+            blocks[l, me, m] = narrow[m]
+        send_along(l, z, True)
+        send_along(l, z, False)
+        cross_copy(l, z).start()
         for index, (src, dst) in enumerate(((mom, mom_out), (params, params_out))):
             copy = pltpu.make_async_copy(src.at[l], dst.at[l], store_sem.at[1 + index, l])
             copy.start()
@@ -174,34 +223,36 @@
 
     load_params.wait()
     load_mom.wait()
-    for step in range(levels + 2):
+    for step in range(levels + 2 + chips):
         if step < levels:
             reduce_level(step)
         if 0 <= step - 1 < levels:
             share_level(step - 1)
         if 0 <= step - 2 < levels:
             update_level(step - 2)
-
-    def waiting2(l, k):
-        source = lax.rem(me + k, n)
-        return pltpu.make_async_remote_copy(
-            chosen.at[l, k], gathered.at[l, :, pl.ds(pl.multiple_of(source * cols, cols), cols)],
-            send2.at[l, k], recv2.at[l, source], device_id={"path": source}, device_id_type=MESH,
-        )
+        for d in range(1, chips):
+            if 0 <= step - 2 - d < levels:
+                relay(step - 2 - d, d)
+        if 0 <= step - 2 - chips < levels:
+            finish_level(step - 2 - chips)
 
     for l in range(levels):
         for k in range(1, n):
-            waiting2(l, k).wait_recv()
-        copy = pltpu.make_async_copy(gathered.at[l], path_out.at[0, l], store_sem.at[3, l])
-        copy.start()
-        stores.append(copy)
-    for l in range(levels):
-        for k in range(1, n):
             waiting1(l, k).wait_send()
-            waiting2(l, k).wait_send()
             path_copy(l, k, 1).wait_send()
         for k in range(1, f):
             fsdp_copy(l, k, 1).wait_send()
+        for owner in range(chips):
+            cross_copy(l, owner).wait_send()
+
+            @pl.when((owner <= z) & (z + 1 < chips))
+            def _():
+                along_copy(l, owner, True).wait_send()
+
+            @pl.when((owner >= z) & (z > 0))
+            def _():
+                along_copy(l, owner, False).wait_send()
+
     for copy in stores:
         copy.wait()
 
@@ -232,7 +283,7 @@
             pltpu.VMEM((levels, rows, depth), bf16),
             pltpu.VMEM((levels, n, rows, cols), bf16),
             pltpu.VMEM(global_params.shape, f32),
-            pltpu.VMEM((levels, n, rows, cols), bf16),
+            pltpu.VMEM((levels, n, 2, rows, cols), bf16),
             pltpu.VMEM((levels, rows, depth), bf16),
             pltpu.VMEM((levels, 2, 128), f32),
             pltpu.VMEM((levels, f, 2, 128), f32),
@@ -242,7 +293,9 @@
             dma((4, levels)),
             dma((levels, n)),
             dma((levels, n)),
-            dma((levels, n)),
+            dma((levels, n // 2)),
+            dma((levels, n // 2)),
+            dma((levels, n // 2)),
             dma((levels, n)),
             dma((levels, f)),
             dma((levels, f)),
@@ -250,7 +303,7 @@
             dma((levels, n)),
         ],
         compiler_params=pltpu.CompilerParams(collective_id=0, has_side_effects=True),
-    )(routes, token_counts, skip_flags, path_delta, feedback, global_params, momentum)
+    )(routes.T, token_counts.T, skip_flags.T, path_delta, feedback, global_params, momentum)
 
 
 def solution(mesh):

time: 68.9 us -> 61.1 us (0.89); the launches traced: 67.7 us -> 60.9 us
  local copies, waits for them, and re-layouts: 9.8 us -> 5.77 us
  Pallas kernels: 57.2 us -> 54.5 us
    unnamed x13 -> x10, local copies, waits for them, and re-layouts: 9.8 us -> 5.77 us
    pallas_call x1, Pallas kernels: 57.2 us -> 54.5 us  [on_device(): pl.pallas_call(functools.partial(kernel, n, f), out_shape=(shape(feedback...]
where the time goes in v2:
time: 61.1 us; the launch traced here: 60.9 us
  Pallas kernels  54.5 us (89%)
  local copies, waits for them, and re-layouts  5.77 us (9%)
  between operations  0.66 us (1%)
    pallas_call x1, Pallas kernels, on_device(): pl.pallas_call(functools.partial(kernel, n, f), out_shape=(shape(feedback...  54.5 us
    unnamed x10, local copies, waits for them, and re-layouts  5.77 us

profile of v2, /device:TPU:1, one launch (start us, length us, event | category | flops | bytes accessed | tf_op | source)
XLA Modules:
  0.0 60.9 jit_solution(1608731607075520248)
XLA Ops:
  0.6 54.5 %shard_map.102 = (f32[1,4,32,4096]{3,2,1,0:T(8,128)}, f32[4,2,32,512]{3,2,1,0:T(8,128)}, f32[4,2,32,512]{3,2,1,0:T(8,128)}, bf16[1,4,32,4096]{3,2,1,0:T(8,128)(2,1)}) custom-call(s32[4,8]{1,0:T(4,128)} %bitcast.3, s32[4,8]{1,0:T(4,128)} %bitcast.4, s32[2,4]{1,0:T(2,128)} %bitcast.5, bf16[1,4,32,4096]{3,2,1,0:T(8,128)(2,1)} %delta_hbm.1, ...), custom_call_target="tpu_custom_call" | custom-call | tf_op jit(solution)/shard_map/pallas_call | solution.py:268
  55.1 0.0 copy-start.2
  55.1 0.0 copy-start.1
  55.1 3.2 %copy.15 = f32[1,4,32,4096]{3,2,1,0:T(8,128)} copy(f32[1,4,32,4096]{3,2,1,0:T(8,128)} %get-tuple-element.8) | data formatting | bytes 4194304
  58.3 0.0 copy-done.2
  58.3 0.0 copy-start
  58.3 0.8 %copy.16 = f32[4,2,32,512]{3,2,1,0:T(8,128)} copy(f32[4,2,32,512]{3,2,1,0:T(8,128)S(1)} %copy-done.2) | data formatting | bytes 1048576
  59.1 0.0 copy-done.1
  59.1 0.8 %copy.17 = f32[4,2,32,512]{3,2,1,0:T(8,128)} copy(f32[4,2,32,512]{3,2,1,0:T(8,128)S(1)} %copy-done.1) | data formatting | bytes 1048576
  59.9 0.0 copy-done
  59.9 1.0 %copy.18 = bf16[1,4,32,4096]{3,2,1,0:T(8,128)(2,1)} copy(bf16[1,4,32,4096]{3,2,1,0:T(8,128)(2,1)S(1)} %copy-done) | data formatting | bytes 2097152
Async XLA Ops:
  55.1 3.2 %copy-start.2 = (f32[4,2,32,512]{3,2,1,0:T(8,128)S(1)}, f32[4,2,32,512]{3,2,1,0:T(8,128)}, u32[]{:S(2)}) copy-start(f32[4,2,32,512]{3,2,1,0:T(8,128)} %get-tuple-element.9) | copy-start | bytes 1572868
  55.1 4.0 %copy-start.1 = (f32[4,2,32,512]{3,2,1,0:T(8,128)S(1)}, f32[4,2,32,512]{3,2,1,0:T(8,128)}, u32[]{:S(2)}) copy-start(f32[4,2,32,512]{3,2,1,0:T(8,128)} %get-tuple-element.10) | copy-start | bytes 1572868
  58.3 1.6 %copy-start = (bf16[1,4,32,4096]{3,2,1,0:T(8,128)(2,1)S(1)}, bf16[1,4,32,4096]{3,2,1,0:T(8,128)(2,1)}, u32[]{:S(2)}) copy-start(bf16[1,4,32,4096]{3,2,1,0:T(8,128)(2,1)} %get-tuple-element.11) | copy-start | bytes 3145732

commit v3 on v2

--- a/solution.py
+++ b/solution.py
@@ -12,6 +12,7 @@
 momentum_coef = 0.9
 epsilon_sq = 1e-06
 MESH = pl.DeviceIdType.MESH
+ahead = 2
 
 
 def kernel(
@@ -49,7 +50,9 @@
         pl.semaphore_signal(barrier, inc=1, device_id={"fsdp": lax.rem(mf + k, f)}, device_id_type=MESH)
 
     inverse = []
-    for l in range(levels):
+    stores = []
+
+    def send_level(l):
         own_route = routes[l, me]
         total = jnp.int32(0)
         for q in range(n):
@@ -78,8 +81,7 @@
                 device_id_type=MESH,
             ).start()
 
-    stores = []
-    for l in range(levels):
+    def feedback_level(l):
         for r in range(0, rows, 16):
             corrected = delta[l, r : r + 16, :].astype(jnp.float32) + feed[l, r : r + 16, :]
             feed[l, r : r + 16, :] = corrected - sent[l, r : r + 16, :].astype(jnp.float32) * inverse[l]
@@ -221,20 +223,26 @@
             copy.start()
             stores.append(copy)
 
+    for l in range(min(ahead, levels)):
+        send_level(l)
+    for l in range(min(ahead, levels)):
+        feedback_level(l)
     load_params.wait()
     load_mom.wait()
-    for step in range(levels + 2 + chips):
+    for step in range(levels + 1 + chips):
         if step < levels:
             reduce_level(step)
+            share_level(step)
+            if step + ahead < levels:
+                send_level(step + ahead)
+                feedback_level(step + ahead)
         if 0 <= step - 1 < levels:
-            share_level(step - 1)
-        if 0 <= step - 2 < levels:
-            update_level(step - 2)
+            update_level(step - 1)
         for d in range(1, chips):
-            if 0 <= step - 2 - d < levels:
-                relay(step - 2 - d, d)
-        if 0 <= step - 2 - chips < levels:
-            finish_level(step - 2 - chips)
+            if 0 <= step - 1 - d < levels:
+                relay(step - 1 - d, d)
+        if 0 <= step - 1 - chips < levels:
+            finish_level(step - 1 - chips)
 
     for l in range(levels):
         for k in range(1, n):

time: 61.1 us -> 60.6 us (level)
  no operation moved by 1% of the time
where the time goes in v3:
time: 60.6 us; the launch traced here: 60.4 us
  Pallas kernels  54 us (89%)
  local copies, waits for them, and re-layouts  5.77 us (10%)
  between operations  0.66 us (1%)
    pallas_call x1, Pallas kernels, on_device(): pl.pallas_call(functools.partial(kernel, n, f), out_shape=(shape(feedback...  54 us
    unnamed x10, local copies, waits for them, and re-layouts  5.77 us

profile of v3, /device:TPU:1, one launch (start us, length us, event | category | flops | bytes accessed | tf_op | source)
XLA Modules:
  0.0 60.4 jit_solution(14805062779889015714)
XLA Ops:
  0.6 54.0 %shard_map.102 = (f32[1,4,32,4096]{3,2,1,0:T(8,128)}, f32[4,2,32,512]{3,2,1,0:T(8,128)}, f32[4,2,32,512]{3,2,1,0:T(8,128)}, bf16[1,4,32,4096]{3,2,1,0:T(8,128)(2,1)}) custom-call(s32[4,8]{1,0:T(4,128)} %bitcast.3, s32[4,8]{1,0:T(4,128)} %bitcast.4, s32[2,4]{1,0:T(2,128)} %bitcast.5, bf16[1,4,32,4096]{3,2,1,0:T(8,128)(2,1)} %delta_hbm.1, ...), custom_call_target="tpu_custom_call" | custom-call | tf_op jit(solution)/shard_map/pallas_call | solution.py:276
  54.6 0.0 copy-start.2
  54.6 0.0 copy-start.1
  54.6 3.2 %copy.15 = f32[1,4,32,4096]{3,2,1,0:T(8,128)} copy(f32[1,4,32,4096]{3,2,1,0:T(8,128)} %get-tuple-element.8) | data formatting | bytes 4194304
  57.8 0.0 copy-done.2
  57.8 0.0 copy-start
  57.8 0.8 %copy.16 = f32[4,2,32,512]{3,2,1,0:T(8,128)} copy(f32[4,2,32,512]{3,2,1,0:T(8,128)S(1)} %copy-done.2) | data formatting | bytes 1048576
  58.6 0.0 copy-done.1
  58.6 0.8 %copy.17 = f32[4,2,32,512]{3,2,1,0:T(8,128)} copy(f32[4,2,32,512]{3,2,1,0:T(8,128)S(1)} %copy-done.1) | data formatting | bytes 1048576
  59.4 0.0 copy-done
  59.4 1.0 %copy.18 = bf16[1,4,32,4096]{3,2,1,0:T(8,128)(2,1)} copy(bf16[1,4,32,4096]{3,2,1,0:T(8,128)(2,1)S(1)} %copy-done) | data formatting | bytes 2097152
Async XLA Ops:
  54.6 3.2 %copy-start.2 = (f32[4,2,32,512]{3,2,1,0:T(8,128)S(1)}, f32[4,2,32,512]{3,2,1,0:T(8,128)}, u32[]{:S(2)}) copy-start(f32[4,2,32,512]{3,2,1,0:T(8,128)} %get-tuple-element.9) | copy-start | bytes 1572868
  54.6 4.0 %copy-start.1 = (f32[4,2,32,512]{3,2,1,0:T(8,128)S(1)}, f32[4,2,32,512]{3,2,1,0:T(8,128)}, u32[]{:S(2)}) copy-start(f32[4,2,32,512]{3,2,1,0:T(8,128)} %get-tuple-element.10) | copy-start | bytes 1572868
  57.8 1.6 %copy-start = (bf16[1,4,32,4096]{3,2,1,0:T(8,128)(2,1)S(1)}, bf16[1,4,32,4096]{3,2,1,0:T(8,128)(2,1)}, u32[]{:S(2)}) copy-start(bf16[1,4,32,4096]{3,2,1,0:T(8,128)(2,1)} %get-tuple-element.11) | copy-start | bytes 3145732

commit v4 on v3

--- a/solution.py
+++ b/solution.py
@@ -229,18 +229,18 @@
         feedback_level(l)
     load_params.wait()
     load_mom.wait()
-    for step in range(levels + 1 + chips):
+    for step in range(levels + 2 + chips):
+        for d in range(chips - 1, 0, -1):
+            if 0 <= step - 1 - d < levels:
+                relay(step - 1 - d, d)
         if step < levels:
             reduce_level(step)
             share_level(step)
-            if step + ahead < levels:
-                send_level(step + ahead)
-                feedback_level(step + ahead)
         if 0 <= step - 1 < levels:
             update_level(step - 1)
-        for d in range(1, chips):
-            if 0 <= step - 1 - d < levels:
-                relay(step - 1 - d, d)
+        if step + ahead < levels:
+            send_level(step + ahead)
+            feedback_level(step + ahead)
         if 0 <= step - 1 - chips < levels:
             finish_level(step - 1 - chips)
 

time: 60.6 us -> 63.4 us (1.046)
  Pallas kernels: 54 us -> 56.8 us
    pallas_call x1, Pallas kernels: 54 us -> 56.8 us  [on_device(): pl.pallas_call(functools.partial(kernel, n, f), out_shape=(shape(feedback...]
where the time goes in v4:
time: 63.4 us; the launch traced here: 63.2 us
  Pallas kernels  56.8 us (90%)
  local copies, waits for them, and re-layouts  5.77 us (9%)
  between operations  0.66 us (1%)
    pallas_call x1, Pallas kernels, on_device(): pl.pallas_call(functools.partial(kernel, n, f), out_shape=(shape(feedback...  56.8 us
    unnamed x10, local copies, waits for them, and re-layouts  5.77 us

profile of v4, /device:TPU:1, one launch (start us, length us, event | category | flops | bytes accessed | tf_op | source)
XLA Modules:
  0.0 63.2 jit_solution(16886209306521936691)
XLA Ops:
  0.6 56.8 %shard_map.102 = (f32[1,4,32,4096]{3,2,1,0:T(8,128)}, f32[4,2,32,512]{3,2,1,0:T(8,128)}, f32[4,2,32,512]{3,2,1,0:T(8,128)}, bf16[1,4,32,4096]{3,2,1,0:T(8,128)(2,1)}) custom-call(s32[4,8]{1,0:T(4,128)} %bitcast.3, s32[4,8]{1,0:T(4,128)} %bitcast.4, s32[2,4]{1,0:T(2,128)} %bitcast.5, bf16[1,4,32,4096]{3,2,1,0:T(8,128)(2,1)} %delta_hbm.1, ...), custom_call_target="tpu_custom_call" | custom-call | tf_op jit(solution)/shard_map/pallas_call | solution.py:276
  57.5 0.0 copy-start.2
  57.5 0.0 copy-start.1
  57.5 3.2 %copy.15 = f32[1,4,32,4096]{3,2,1,0:T(8,128)} copy(f32[1,4,32,4096]{3,2,1,0:T(8,128)} %get-tuple-element.8) | data formatting | bytes 4194304
  60.7 0.0 copy-done.2
  60.7 0.0 copy-start
  60.7 0.8 %copy.16 = f32[4,2,32,512]{3,2,1,0:T(8,128)} copy(f32[4,2,32,512]{3,2,1,0:T(8,128)S(1)} %copy-done.2) | data formatting | bytes 1048576
  61.5 0.0 copy-done.1
  61.5 0.8 %copy.17 = f32[4,2,32,512]{3,2,1,0:T(8,128)} copy(f32[4,2,32,512]{3,2,1,0:T(8,128)S(1)} %copy-done.1) | data formatting | bytes 1048576
  62.3 0.0 copy-done
  62.3 1.0 %copy.18 = bf16[1,4,32,4096]{3,2,1,0:T(8,128)(2,1)} copy(bf16[1,4,32,4096]{3,2,1,0:T(8,128)(2,1)S(1)} %copy-done) | data formatting | bytes 2097152
Async XLA Ops:
  57.5 3.2 %copy-start.2 = (f32[4,2,32,512]{3,2,1,0:T(8,128)S(1)}, f32[4,2,32,512]{3,2,1,0:T(8,128)}, u32[]{:S(2)}) copy-start(f32[4,2,32,512]{3,2,1,0:T(8,128)} %get-tuple-element.9) | copy-start | bytes 1572868
  57.5 4.0 %copy-start.1 = (f32[4,2,32,512]{3,2,1,0:T(8,128)S(1)}, f32[4,2,32,512]{3,2,1,0:T(8,128)}, u32[]{:S(2)}) copy-start(f32[4,2,32,512]{3,2,1,0:T(8,128)} %get-tuple-element.10) | copy-start | bytes 1572868
  60.7 1.6 %copy-start = (bf16[1,4,32,4096]{3,2,1,0:T(8,128)(2,1)S(1)}, bf16[1,4,32,4096]{3,2,1,0:T(8,128)(2,1)}, u32[]{:S(2)}) copy-start(bf16[1,4,32,4096]{3,2,1,0:T(8,128)(2,1)} %get-tuple-element.11) | copy-start | bytes 3145732

commit v5 on v3

--- a/solution.py
+++ b/solution.py
@@ -310,7 +310,7 @@
             dma((levels, n)),
             dma((levels, n)),
         ],
-        compiler_params=pltpu.CompilerParams(collective_id=0, has_side_effects=True),
+        compiler_params=pltpu.CompilerParams(collective_id=0, has_side_effects=True, vmem_limit_bytes=46 * 1024 * 1024),
     )(routes.T, token_counts.T, skip_flags.T, path_delta, feedback, global_params, momentum)
 
 

time: 60.6 us -> 63.6 us (1.050)
  local copies, waits for them, and re-layouts: 5.77 us -> 9.22 us
    unnamed x10 -> x16, local copies, waits for them, and re-layouts: 5.77 us -> 9.22 us
where the time goes in v5:
time: 63.6 us; the launch traced here: 63.3 us
  Pallas kernels  53.4 us (84%)
  local copies, waits for them, and re-layouts  9.22 us (14%)
  between operations  0.66 us (1%)
    pallas_call x1, Pallas kernels, on_device(): pl.pallas_call(functools.partial(kernel, n, f), out_shape=(shape(feedback...  53.4 us
    unnamed x16, local copies, waits for them, and re-layouts  9.22 us

profile of v5, /device:TPU:1, one launch (start us, length us, event | category | flops | bytes accessed | tf_op | source)
XLA Modules:
  0.0 63.3 jit_solution(6496113282090679836)
XLA Ops:
  0.6 0.0 copy-start
  0.6 1.2 %copy-done = bf16[1,4,32,4096]{3,2,1,0:T(8,128)(2,1)S(1)} copy-done((bf16[1,4,32,4096]{3,2,1,0:T(8,128)(2,1)S(1)}, bf16[1,4,32,4096]{3,2,1,0:T(8,128)(2,1)}, u32[]{:S(2)}) %copy-start) | copy-done | bytes 1048600
  1.9 0.0 copy-start.1
  1.9 1.0 %copy-done.1 = f32[4,2,32,512]{3,2,1,0:T(8,128)S(1)} copy-done((f32[4,2,32,512]{3,2,1,0:T(8,128)S(1)}, f32[4,2,32,512]{3,2,1,0:T(8,128)}, u32[]{:S(2)}) %copy-start.1) | copy-done | bytes 524312
  2.9 0.0 copy-start.2
  2.9 1.0 %copy-done.2 = f32[4,2,32,512]{3,2,1,0:T(8,128)S(1)} copy-done((f32[4,2,32,512]{3,2,1,0:T(8,128)S(1)}, f32[4,2,32,512]{3,2,1,0:T(8,128)}, u32[]{:S(2)}) %copy-start.2) | copy-done | bytes 524312
  3.9 0.0 copy-start.3
  3.9 0.7 %copy-done.3 = s32[8,4]{0,1:T(4,128)S(1)} copy-done((s32[8,4]{0,1:T(4,128)S(1)}, s32[8,4]{0,1:T(4,128)}, u32[]{:S(2)}) %copy-start.3) | copy-done | bytes 152
  4.6 0.0 copy-start.4
  4.6 0.7 %copy-done.4 = s32[8,4]{0,1:T(4,128)S(1)} copy-done((s32[8,4]{0,1:T(4,128)S(1)}, s32[8,4]{0,1:T(4,128)}, u32[]{:S(2)}) %copy-start.4) | copy-done | bytes 152
  5.3 0.0 copy-start.5
  5.3 0.7 %copy-done.5 = s32[4,2]{0,1:T(2,128)S(1)} copy-done((s32[4,2]{0,1:T(2,128)S(1)}, s32[4,2]{0,1:T(2,128)}, u32[]{:S(2)}) %copy-start.5) | copy-done | bytes 56
  6.0 53.4 %shard_map.102 = (f32[1,4,32,4096]{3,2,1,0:T(8,128)S(1)}, f32[4,2,32,512]{3,2,1,0:T(8,128)S(1)}, f32[4,2,32,512]{3,2,1,0:T(8,128)S(1)}, bf16[1,4,32,4096]{3,2,1,0:T(8,128)(2,1)S(1)}) custom-call(s32[4,8]{1,0:T(4,128)S(1)} %bitcast.3, s32[4,8]{1,0:T(4,128)S(1)} %bitcast.4, s32[2,4]{1,0:T(2,128)S(1)} %bitcast.5, bf16[1,4,32,4096]{3,2,1,0:T(8,128)(2,1)S(1)} %copy-done, ...), custom_call_target="tpu_custom_call" | custom-call | tf_op jit(solution)/shard_map/pallas_call | solution.py:276
  59.4 1.3 %copy.15 = f32[1,4,32,4096]{3,2,1,0:T(8,128)} copy(f32[1,4,32,4096]{3,2,1,0:T(8,128)S(1)} %get-tuple-element.8) | data formatting | bytes 4194304
  60.7 0.8 %copy.16 = f32[4,2,32,512]{3,2,1,0:T(8,128)} copy(f32[4,2,32,512]{3,2,1,0:T(8,128)S(1)} %get-tuple-element.9) | data formatting | bytes 1048576
  61.5 0.8 %copy.17 = f32[4,2,32,512]{3,2,1,0:T(8,128)} copy(f32[4,2,32,512]{3,2,1,0:T(8,128)S(1)} %get-tuple-element.10) | data formatting | bytes 1048576
  62.3 1.0 %copy.18 = bf16[1,4,32,4096]{3,2,1,0:T(8,128)(2,1)} copy(bf16[1,4,32,4096]{3,2,1,0:T(8,128)(2,1)S(1)} %get-tuple-element.11) | data formatting | bytes 2097152
Async XLA Ops:
  0.6 1.2 %copy-start = (bf16[1,4,32,4096]{3,2,1,0:T(8,128)(2,1)S(1)}, bf16[1,4,32,4096]{3,2,1,0:T(8,128)(2,1)}, u32[]{:S(2)}) copy-start(bf16[1,4,32,4096]{3,2,1,0:T(8,128)(2,1)} %delta_hbm.1) | copy-start | bytes 3145732
  1.9 1.0 %copy-start.1 = (f32[4,2,32,512]{3,2,1,0:T(8,128)S(1)}, f32[4,2,32,512]{3,2,1,0:T(8,128)}, u32[]{:S(2)}) copy-start(f32[4,2,32,512]{3,2,1,0:T(8,128)} %params_hbm.1) | copy-start | bytes 1572868
  2.9 1.0 %copy-start.2 = (f32[4,2,32,512]{3,2,1,0:T(8,128)S(1)}, f32[4,2,32,512]{3,2,1,0:T(8,128)}, u32[]{:S(2)}) copy-start(f32[4,2,32,512]{3,2,1,0:T(8,128)} %mom_hbm.1) | copy-start | bytes 1572868
  3.9 0.7 %copy-start.3 = (s32[8,4]{0,1:T(4,128)S(1)}, s32[8,4]{0,1:T(4,128)}, u32[]{:S(2)}) copy-start(s32[8,4]{0,1:T(4,128)} %param.11) | copy-start | bytes 388
  4.6 0.7 %copy-start.4 = (s32[8,4]{0,1:T(4,128)S(1)}, s32[8,4]{0,1:T(4,128)}, u32[]{:S(2)}) copy-start(s32[8,4]{0,1:T(4,128)} %param.12) | copy-start | bytes 388
  5.3 0.7 %copy-start.5 = (s32[4,2]{0,1:T(2,128)S(1)}, s32[4,2]{0,1:T(2,128)}, u32[]{:S(2)}) copy-start(s32[4,2]{0,1:T(2,128)} %param.13) | copy-start | bytes 100

commit v6 on v3

--- a/solution.py
+++ b/solution.py
@@ -12,7 +12,7 @@
 momentum_coef = 0.9
 epsilon_sq = 1e-06
 MESH = pl.DeviceIdType.MESH
-ahead = 2
+ahead = 3
 
 
 def kernel(

time: 60.6 us -> 61.1 us (level)
  no operation moved by 1% of the time
where the time goes in v6:
time: 61.1 us; the launch traced here: 60.9 us
  Pallas kernels  54.5 us (89%)
  local copies, waits for them, and re-layouts  5.77 us (9%)
  between operations  0.66 us (1%)
    pallas_call x1, Pallas kernels, on_device(): pl.pallas_call(functools.partial(kernel, n, f), out_shape=(shape(feedback...  54.5 us
    unnamed x10, local copies, waits for them, and re-layouts  5.77 us

profile of v6, /device:TPU:1, one launch (start us, length us, event | category | flops | bytes accessed | tf_op | source)
XLA Modules:
  0.0 60.9 jit_solution(4348440509558493793)
XLA Ops:
  0.6 54.5 %shard_map.102 = (f32[1,4,32,4096]{3,2,1,0:T(8,128)}, f32[4,2,32,512]{3,2,1,0:T(8,128)}, f32[4,2,32,512]{3,2,1,0:T(8,128)}, bf16[1,4,32,4096]{3,2,1,0:T(8,128)(2,1)}) custom-call(s32[4,8]{1,0:T(4,128)} %bitcast.3, s32[4,8]{1,0:T(4,128)} %bitcast.4, s32[2,4]{1,0:T(2,128)} %bitcast.5, bf16[1,4,32,4096]{3,2,1,0:T(8,128)(2,1)} %delta_hbm.1, ...), custom_call_target="tpu_custom_call" | custom-call | tf_op jit(solution)/shard_map/pallas_call | solution.py:276
  55.1 0.0 copy-start.2
  55.1 0.0 copy-start.1
  55.2 3.2 %copy.15 = f32[1,4,32,4096]{3,2,1,0:T(8,128)} copy(f32[1,4,32,4096]{3,2,1,0:T(8,128)} %get-tuple-element.8) | data formatting | bytes 4194304
  58.4 0.0 copy-done.2
  58.4 0.0 copy-start
  58.4 0.8 %copy.16 = f32[4,2,32,512]{3,2,1,0:T(8,128)} copy(f32[4,2,32,512]{3,2,1,0:T(8,128)S(1)} %copy-done.2) | data formatting | bytes 1048576
  59.2 0.0 copy-done.1
  59.2 0.8 %copy.17 = f32[4,2,32,512]{3,2,1,0:T(8,128)} copy(f32[4,2,32,512]{3,2,1,0:T(8,128)S(1)} %copy-done.1) | data formatting | bytes 1048576
  60.0 0.0 copy-done
  60.0 1.0 %copy.18 = bf16[1,4,32,4096]{3,2,1,0:T(8,128)(2,1)} copy(bf16[1,4,32,4096]{3,2,1,0:T(8,128)(2,1)S(1)} %copy-done) | data formatting | bytes 2097152
Async XLA Ops:
  55.1 3.2 %copy-start.2 = (f32[4,2,32,512]{3,2,1,0:T(8,128)S(1)}, f32[4,2,32,512]{3,2,1,0:T(8,128)}, u32[]{:S(2)}) copy-start(f32[4,2,32,512]{3,2,1,0:T(8,128)} %get-tuple-element.9) | copy-start | bytes 1572868
  55.1 4.0 %copy-start.1 = (f32[4,2,32,512]{3,2,1,0:T(8,128)S(1)}, f32[4,2,32,512]{3,2,1,0:T(8,128)}, u32[]{:S(2)}) copy-start(f32[4,2,32,512]{3,2,1,0:T(8,128)} %get-tuple-element.10) | copy-start | bytes 1572868
  58.4 1.6 %copy-start = (bf16[1,4,32,4096]{3,2,1,0:T(8,128)(2,1)S(1)}, bf16[1,4,32,4096]{3,2,1,0:T(8,128)(2,1)}, u32[]{:S(2)}) copy-start(bf16[1,4,32,4096]{3,2,1,0:T(8,128)(2,1)} %get-tuple-element.11) | copy-start | bytes 3145732
